TPU v7x, 32 devices: a whole 2x2x4 slice. The times are simulated.
32 devices in a mesh: section: 8 (over y, x, core), tensor: 4 (over z).
Axes of the slice: x: 2, y: 2, z: 4, core: 2. Of those that a mesh axis runs over, the one named last changes fastest.
Arguments:
- states: bfloat16 [4096, 8192], P('section', 'tensor'), may hold values from -6 to 6
- lengths: int32 [8, 16], P('section'), may hold values from 1 to 96, 512 in all within a row
- routes: int32 [4096, 1], P('section'), may hold values from 0 to 7; in each aligned block of 512 rows (0 to 511, 512 to 1023, ...) at most 128 rows name the same one
- score_gain: float32 [8, 8192], P('section'), may hold values from 0.25 to 1.75
- score_weight: bfloat16 [8, 8192, 4096], P('section', None, 'tensor'), may hold values from -0.0625 to 0.0625
- score_heads: float32 [8, 4096, 2], P('section', 'tensor'), may hold values from -0.09375 to 0.09375
- actor_gain: float32 [8192], replicated, may hold values from 0.25 to 1.75
- actor_weight: bfloat16 [8192, 4096], P(None, 'tensor'), may hold values from -0.0625 to 0.0625
- actor_heads: float32 [4096], P('tensor'), may hold values from -0.09375 to 0.09375
Outputs:
- packed_scores: float32 [2, 8192], P(None, 'section')
- advantages: float32 [4096], P('section')
- actor_grad: float32 [8192, 4096], P('section', 'tensor')
Inputs may be any that keep to these rules, and one draw needn't show every extreme that they name: `lengths`: each row sums to 512; its largest entry is exactly 96. `routes`: in the rows of one section (aligned blocks of 512 rows) no member is named by more than 128 rows; some member is named by exactly 128 rows of some block.
All inputs are finite; a program needn't handle non-finite values.
Results may differ from a plain program's by a relative error of at most 0.0055.
Values may be sent and summed in bfloat16 or wider, within the bound.
A program may use at most 128 MiB of HBM per device.

v0:
```python
import jax
import jax.numpy as jnp
from jax import lax
from jax.sharding import PartitionSpec as P

epsilon = 1e-05
trace_decay = 0.95
penalty = 0.1


def compose(earlier, later):
    return (earlier[0] * later[0], later[1] + later[0] * earlier[1])


def advantage_rows(values, rewards, lengths):
    ends = jnp.cumsum(lengths, axis=1) - 1
    steps_idx = jnp.arange(values.shape[1], dtype=jnp.int32)
    last = jnp.any(steps_idx[None, :, None] == ends[:, None, :], axis=2)
    following = jnp.concatenate([values[:, 1:], jnp.zeros_like(values[:, :1])], axis=1)
    delta = jnp.where(last, rewards, following) - values
    weight = jnp.where(last, 0.0, trace_decay).astype(values.dtype)
    carried = lax.associative_scan(compose, (weight[:, ::-1], delta[:, ::-1]), axis=1)
    return carried[1][:, ::-1]


def body(
    states,
    lengths,
    routes,
    score_gain,
    score_weight,
    score_heads,
    actor_gain,
    actor_weight,
    actor_heads,
):
    sections = lax.axis_size("section")
    tok_count = states.shape[0]
    feat_shard = states.shape[1]
    capacity = 2 * tok_count // sections
    slot_count = sections * capacity
    target = routes[:, 0]
    onehot = (target[:, None] == jnp.arange(sections, dtype=jnp.int32)[None, :]).astype(jnp.int32)
    before = jnp.cumsum(onehot, axis=0) - onehot
    placed = jnp.sum(before * onehot, axis=1)
    slot_index = target * capacity + placed
    dispatch = (jnp.arange(slot_count, dtype=jnp.int32)[:, None] == slot_index[None, :]).astype(
        jnp.bfloat16
    )
    outbox = jnp.dot(dispatch, states, preferred_element_type=jnp.float32).astype(jnp.bfloat16)
    outbox = outbox.reshape(sections, capacity, feat_shard)
    arrived = lax.all_to_all(outbox, "section", split_axis=0, concat_axis=0, tiled=True).reshape(
        slot_count, feat_shard
    )
    gain_row = score_gain[0]
    member_weight = score_weight[0]
    feat_width = gain_row.shape[0]
    widened = lax.all_gather(arrived, "tensor", axis=1, tiled=True).astype(jnp.float32)
    scaled = (widened * gain_row[None, :]).astype(jnp.bfloat16)
    acc_total = jnp.dot(scaled, member_weight, preferred_element_type=jnp.float32)
    acc_total, squares = (acc_total, jnp.sum(widened * widened, axis=1))
    member_scale = lax.rsqrt(squares / feat_width + epsilon)
    preact = acc_total * member_scale[:, None]
    partial_scores = jnp.dot(jax.nn.silu(preact), score_heads[0], precision=lax.Precision.HIGHEST)
    scores = lax.psum(partial_scores, "tensor")
    packed_scores = jnp.transpose(scores)
    returned = lax.all_to_all(
        scores.reshape(sections, capacity, 2), "section", split_axis=0, concat_axis=0, tiled=True
    )
    returned = returned.reshape(slot_count, 2)
    token_scores = jnp.take(returned, slot_index, axis=0)
    raw_adv = advantage_rows(token_scores[:, 0][None, :], token_scores[:, 1][None, :], lengths)[0]
    adv_total, adv_square = lax.psum((jnp.sum(raw_adv), jnp.sum(raw_adv * raw_adv)), "section")
    total_tokens = tok_count * sections
    center = adv_total / total_tokens
    spread = adv_square / total_tokens - center * center
    advantages = (raw_adv - center) * lax.rsqrt(spread + epsilon)
    features = lax.all_gather(states, "tensor", axis=1, tiled=True)
    widened = features.astype(jnp.float32)
    actor_scale = lax.rsqrt(jnp.mean(widened * widened, axis=1) + epsilon)
    gained = (widened * actor_gain[None, :]).astype(jnp.bfloat16)
    actor_pre = (
        jnp.dot(gained, actor_weight, preferred_element_type=jnp.float32) * actor_scale[:, None]
    )
    shift_part = jnp.dot(jax.nn.silu(actor_pre), actor_heads, precision=lax.Precision.HIGHEST)
    log_shift = lax.psum(shift_part, "tensor")
    ratios = jnp.exp(log_shift)
    logit_slope = penalty * (ratios - 1.0) - ratios * advantages
    sigmoid_pre = jax.nn.sigmoid(actor_pre)
    silu_slope = sigmoid_pre * (1.0 + actor_pre * (1.0 - sigmoid_pre))
    grad_pre = ((logit_slope * actor_scale)[:, None] * actor_heads[None, :] * silu_slope).astype(
        jnp.bfloat16
    )
    blocks = lax.all_to_all(gained, "section", split_axis=1, concat_axis=0, tiled=True)
    every_row = lax.all_gather(grad_pre, "section", axis=0, tiled=True)
    actor_grad = lax.dot_general(
        blocks, every_row, (((0,), (0,)), ((), ())), preferred_element_type=jnp.float32
    )
    return (packed_scores, advantages, actor_grad)


def solution(mesh):
    in_specs = (
        P("section", "tensor"),
        P("section", None),
        P("section", None),
        P("section", None),
        P("section", None, "tensor"),
        P("section", "tensor", None),
        P(),
        P(None, "tensor"),
        P("tensor"),
    )
    out_specs = (P(None, "section"), P("section"), P("section", "tensor"))
    return jax.shard_map(body, mesh=mesh, in_specs=in_specs, out_specs=out_specs, check_vma=False)
```

profile of v0, /device:TPU:0, one launch (start us, length us, event | category | flops | bytes accessed | tf_op | source)
XLA Modules:
  0.0 717.2 jit_solution(90734786162934419)
XLA Ops:
  7.2 4.1 copy.28
  11.4 1.1 reduce-window.14
  12.9 2.4 convolution_convert_fusion
  15.3 54.1 %all_to_all.29 = bf16[8,128,2048]{2,1,0:T(8,128)(2,1)} all-to-all(bf16[8,128,2048]{2,1,0:T(8,128)(2,1)S(1)} %bitcast.52), channel_id=1, replica_groups=mesh['section'=8,'tensor'=4] {'section'}, dimensions={0} | all-to-all | bytes 8388608 | tf_op jit(solution)/shard_map/all_to_all | solution.py:52
  70.4 93.4 %all-gather.6.cloned.1.call-done = bf16[512,8192]{0,1:T(8,128)(2,1)} async-done(((bf16[512,2048]{0,1:T(8,128)(2,1)}), bf16[512,8192]{0,1:T(8,128)(2,1)}) %all-gather.6.cloned.1.call-update) | async-done | bytes 8388624 | tf_op jit(solution)/shard_map/all_gather | solution.py:78
  163.8 5.2 fusion.3
  169.1 15.5 %fusion.43 = f32[512,1024]{1,0:T(8,128)S(1)} fusion(bf16[512,8192]{0,1:T(8,128)(2,1)S(1)} %get-tuple-element.14, bf16[8192,1024]{1,0:T(8,128)(2,1)} %param.16), kind=kOutput, calls=%fused_computation.95 | convolution fusion | flops 8589934592 | bytes 27262976 | tf_op jit(solution)/shard_map/dot_general | solution.py:83
  184.6 2.4 fusion.15
  187.0 263.4 %all-gather.4.cloned.1.call-done = bf16[1024,8192]{1,0:T(8,128)(2,1)} async-done(((bf16[1024,2048]{1,0:T(8,128)(2,1)}), bf16[1024,8192]{1,0:T(8,128)(2,1)}) %all-gather.4.cloned.1.call-update) | async-done | bytes 16777232 | tf_op jit(solution)/shard_map/all_gather | solution.py:58
  450.4 7.5 %fusion.1 = f32[1024]{0:T(1024)S(1)} fusion(bf16[1024,8192]{1,0:T(8,128)(2,1)} %all-gather.4.cloned.1.call-done), kind=kLoop, calls=%fused_computation.4 | loop fusion | flops 25164800 | bytes 16781312 | tf_op jit(solution)/shard_map/reduce_sum | solution.py:61
  457.9 3.1 copy-done.2
  461.0 21.0 %fusion.4 = f32[1024,1024]{1,0:T(8,128)S(1)} fusion(bf16[1024,8192]{1,0:T(8,128)(2,1)S(1)} %copy-done.2, bf16[1,8192,1024]{2,1,0:T(8,128)(2,1)} %param.13, f32[8192]{0:T(1024)S(1)} %bitcast.73), kind=kOutput, calls=%fused_computation.9 | convolution fusion | flops 17205035008 | bytes 37781504 | tf_op jit(solution)/shard_map/dot_general | solution.py:60
  482.1 4.5 fusion.8
  486.6 16.3 %all-reduce.19 = (f32[1024,2]{0,1:T(2,128)}, f32[512]{0:T(512)S(1)}) all-reduce(f32[1024,2]{0,1:T(2,128)S(1)} %fusion.8, f32[512]{0:T(512)S(1)} %bitcast.66), channel_id=1, replica_groups=mesh['section'=8,'tensor'=4] {'tensor'}, use_global_device_ids=true, to_apply=%region_4.5 | all-reduce | flops 2560 | bytes 20480 | tf_op jit(solution)/shard_map/psum | solution.py:65
  502.8 3.9 all-to-all-start.1
  506.8 4.7 all-to-all-done.1
  511.6 1.0 gather_fusion
  528.3 0.7 pad_maximum_fusion.1
  532.3 0.7 pad_maximum_fusion
  534.5 12.7 %all-reduce.18 = (f32[]{:T(128)}, f32[]{:T(128)}) all-reduce(f32[]{:T(128)} %get-tuple-element.6, f32[]{:T(128)} %get-tuple-element.5), channel_id=1, replica_groups=mesh['section'=8,'tensor'=4] {'section'}, use_global_device_ids=true, to_apply=%region_10.11 | all-reduce | flops 2 | bytes 16 | tf_op jit(solution)/shard_map/psum | solution.py:73
  549.8 1.9 multiply_convert_fusion
  551.7 132.4 %all_to_all.30 = bf16[512,8,1024]{0,2,1:T(8,128)(2,1)} all-to-all(bf16[512,8,1024]{0,2,1:T(8,128)(2,1)} %bitcast.47), channel_id=1, replica_groups=mesh['section'=8,'tensor'=4] {'section'}, dimensions={1} | all-to-all | bytes 16777216 | tf_op jit(solution)/shard_map/all_to_all | solution.py:94
  684.1 11.5 %copy.29 = bf16[8,512,1024]{2,1,0:T(8,128)(2,1)} copy(bf16[8,512,1024]{1,2,0:T(8,128)(2,1)} %bitcast.48) | data formatting | bytes 16777216 | tf_op jit(solution)/shard_map/all_to_all | solution.py:94
  695.6 15.0 %fusion.44 = f32[1024,1024]{1,0:T(8,128)} fusion(bf16[4096,1024]{1,0:T(8,128)(2,1)} %bitcast.51, bf16[4096,1024]{1,0:T(8,128)(2,1)} %all-gather.8.cloned.1.call-done), kind=kOutput, calls=%fused_computation.96 | convolution fusion | flops 8589934592 | bytes 20971520 | tf_op jit(solution)/shard_map/dot_general | solution.py:96
  (153 shorter events, 18.8 us)
Async XLA Ops:
  7.2 474.9 %copy-start = (f32[1,1024,2]{1,2,0:T(2,128)S(1)}, f32[1,1024,2]{1,2,0:T(2,128)}, u32[]{:S(2)}) copy-start(f32[1,1024,2]{1,2,0:T(2,128)} %param.14) | copy-start | bytes 24580
  7.2 5.7 copy-start.3
  7.2 4.2 copy-start.5
  7.2 156.6 %all-gather.6.cloned.1.call-start = ((), (), s32[]{:S(2)}) async-start(), calls=%async_computation.4 | async-start | bytes 10485760 | tf_op jit(solution)/shard_map/all_gather | solution.py:78
  11.3 439.0 %all-gather.4.cloned.1.call-start = ((), (), s32[]{:S(2)}) async-start(), calls=%async_computation.3 | async-start | bytes 20971520 | tf_op jit(solution)/shard_map/all_gather | solution.py:58
  69.4 0.7 copy-start.8
  69.4 94.4 %copy-start.4 = (f32[8192]{0:T(1024)S(1)}, f32[8192]{0:T(1024)}, u32[]{:S(2)}) copy-start(f32[8192]{0:T(1024)} %param.15) | copy-start | bytes 98308
  169.1 15.5 %copy-start.1 = (bf16[512,8192]{0,1:T(8,128)(2,1)}, bf16[512,8192]{0,1:T(8,128)(2,1)S(1)}, u32[]{:S(2)}) copy-start(bf16[512,8192]{0,1:T(8,128)(2,1)S(1)} %get-tuple-element.14) | copy-start | bytes 25165828
  169.1 15.5 %copy-start.7 = (f32[1024]{0:T(1024)S(1)}, f32[1024]{0:T(1024)}, u32[]{:S(2)}) copy-start(f32[1024]{0:T(1024)} %param.17) | copy-start | bytes 12292
  184.6 273.3 %copy-start.9 = (f32[1,8192]{1,0:T(1,128)S(1)}, f32[1,8192]{1,0:T(1,128)}, u32[]{:S(2)}) copy-start(f32[1,8192]{1,0:T(1,128)} %param.12) | copy-start | bytes 98308
  450.4 10.7 %copy-start.2 = (bf16[1024,8192]{1,0:T(8,128)(2,1)S(1)}, bf16[1024,8192]{1,0:T(8,128)(2,1)}, u32[]{:S(2)}) copy-start(bf16[1024,8192]{1,0:T(8,128)(2,1)} %all-gather.4.cloned.1.call-done) | copy-start | bytes 50331652
  502.8 8.6 %all-to-all-start.1 = ((f32[8,128,2]{1,2,0:T(2,128)}), f32[8,128,2]{1,2,0:T(2,128)S(1)}, u32[]{:S(2)}, u32[]{:S(2)}) async-start(f32[8,128,2]{1,2,0:T(2,128)} %bitcast.12), calls=%async_computation.1 | async-start | bytes 16384 | tf_op jit(solution)/shard_map/all_to_all | solution.py:67
  506.7 188.9 %all-gather.8.cloned.1.call-start = ((), (), s32[]{:S(2)}) async-start(), calls=%async_computation.5 | async-start | bytes 9437184 | tf_op jit(solution)/shard_map/all_gather | solution.py:95
  549.8 134.4 %copy-start.6 = (f32[1,512]{1,0:T(1,128)}, f32[1,512]{1,0:T(1,128)S(1)}, u32[]{:S(2)}) copy-start(f32[1,512]{1,0:T(1,128)S(1)} %subtract_multiply_fusion.1) | copy-start | bytes 6148
Sparse Core Ops, SparseCore 0:
  11.5 152.3 all-gather.5
  165.4 284.9 all-gather.3
  551.8 119.5 all-gather.7
where the time goes:
time: 718 us; the launch traced here: 717 us
  waiting for transfers between devices  361 us (50%)
  blocking collectives  215 us (30%)
  matrix products  60.8 us (8%)
  local copies, waits for them, and re-layouts  35 us (5%)
  other arithmetic  20.5 us (3%)
  between operations  20 us (3%)
    all_gather x1, waiting for transfers between devices, body(): lax.all_gather(arrived, 'tensor', axis=1, tiled=True).astype(jnp.float32)  263 us
    all_to_all x1, blocking collectives, body(): lax.all_to_all(gained, 'section', split_axis=1, concat_axis=0, tiled=True)  132 us
    all_gather x1, waiting for transfers between devices, body(): features = lax.all_gather(states, 'tensor', axis=1, tiled=True)  93.4 us
    all_to_all x1, blocking collectives, body(): lax.all_to_all(outbox, 'section', split_axis=0, concat_axis=0, tiled=True)  54.1 us
    dot_general x1, matrix products, body(): jnp.dot(scaled, member_weight, preferred_element_type=jnp.float32)  21 us
    psum x1, blocking collectives, body(): scores = lax.psum(partial_scores, 'tensor')  16.3 us
    dot_general x1, matrix products, body(): jnp.dot(gained, actor_weight, preferred_element_type=jnp.float32)  15.5 us
    dot_general x1, matrix products, body(): lax.dot_general(blocks, every_row, (((0,), (0,)), ((), ())), preferred_el...  15 us
  transfers between devices with their start and end apart: 4, of which 3 were waited for; matrix products, arithmetic and copies ran while one was open for 5% of the time, Pallas kernels for 0%

commit v1 on v0

v1 whole, which is shorter than its diff:
```python
import functools
import jax
import jax.numpy as jnp
from jax import lax
from jax.experimental import pallas as pl
from jax.experimental.pallas import tpu as pltpu
from jax.sharding import PartitionSpec as P

epsilon = 1e-05
trace_decay = 0.95
penalty = 0.1
MESH = pl.DeviceIdType.MESH


def exchange(
    sections, tensors, cap,
    states, dispatch, gain_m, gain_a, weight_m, weight_a,
    acc_m, acc_a, sq_m, sq_a, blocks,
    feats, outbox, inbox, work, wbuf_m, wbuf_a,
    z_send, z_recv, m_send, m_recv, b_send, b_recv, loc_sem, w_sem,
):
    s = lax.axis_index("section")
    t = lax.axis_index("tensor")
    tok, fs = states.shape
    slots = sections * cap
    bps = sections // tensors
    bw = fs // bps
    hid = acc_m.shape[1]
    nt = min(hid, 256)
    chunks = 2
    half = tok // chunks
    up_ok = t + 1 < tensors
    dn_ok = t > 0

    load = pltpu.make_async_copy(states, feats.at[t], loc_sem.at[0])
    load.start()

    barrier = pltpu.get_barrier_semaphore()

    def greet(r, c):
        pl.semaphore_signal(barrier, inc=1, device_id=(lax.rem(s + r, sections), t), device_id_type=MESH)
        return c

    lax.fori_loop(1, sections, greet, 0)

    @pl.when(up_ok)
    def _():
        pl.semaphore_signal(barrier, inc=1, device_id=(s, t + 1), device_id_type=MESH)

    @pl.when(dn_ok)
    def _():
        pl.semaphore_signal(barrier, inc=1, device_id=(s, t - 1), device_id_type=MESH)

    peers = sections - 1 + jnp.where(up_ok, 1, 0) + jnp.where(dn_ok, 1, 0)
    pl.semaphore_wait(barrier, peers)

    acc_m[...] = jnp.zeros_like(acc_m)
    acc_a[...] = jnp.zeros_like(acc_a)
    sq_m[...] = jnp.zeros_like(sq_m)
    sq_a[...] = jnp.zeros_like(sq_a)
    load.wait()

    def z_copy(way, hop, c, shard, dest):
        rows = pl.ds(c * half, half)
        return pltpu.make_async_remote_copy(
            src_ref=feats.at[shard, rows], dst_ref=feats.at[shard, rows],
            send_sem=z_send.at[way, hop, c], recv_sem=z_recv.at[way, hop, c],
            device_id=(s, dest), device_id_type=MESH,
        )

    def m_copy(k, dest, src):
        return pltpu.make_async_remote_copy(
            src_ref=outbox.at[k, pl.ds(pl.multiple_of(dest * cap, cap), cap)],
            dst_ref=inbox.at[k, pl.ds(pl.multiple_of(src * cap, cap), cap)],
            send_sem=m_send.at[k, dest], recv_sem=m_recv.at[k, src],
            device_id=(dest, t), device_id_type=MESH,
        )

    def b_src(dest):
        return feats.at[dest // bps, :, pl.ds(pl.multiple_of(lax.rem(dest, bps) * bw, bw), bw)]

    def b_copy(dest, src):
        return pltpu.make_async_remote_copy(
            src_ref=b_src(dest), dst_ref=blocks.at[src],
            send_sem=b_send.at[dest], recv_sem=b_recv.at[src],
            device_id=(dest, t), device_id_type=MESH,
        )

    def own_copy(k):
        rows = pl.ds(pl.multiple_of(s * cap, cap), cap)
        return pltpu.make_async_copy(outbox.at[k, rows], inbox.at[k, rows], m_recv.at[k, s])

    def w_copy(weight, buf, which, k):
        return pltpu.make_async_copy(
            weight.at[pl.ds(pl.multiple_of(k * fs, fs), fs)], buf, w_sem.at[which]
        )

    rb = 64

    def scale_rows(read, write, sq, gain, rows):
        def step(i, c):
            rr = pl.ds(pl.multiple_of(i * rb, rb), rb)
            x = read(rr).astype(jnp.float32)
            part = x * x
            total = part[:, 0:128]
            for j in range(1, fs // 128):
                total = total + part[:, j * 128:(j + 1) * 128]
            sq[rr, :] += total
            write(rr, (x * gain).astype(jnp.bfloat16))
            return c
        lax.fori_loop(0, rows // rb, step, 0)

    def accumulate(acc, left, buf):
        def step(n, c):
            cols = pl.ds(pl.multiple_of(n * nt, nt), nt)
            acc[:, cols] += jnp.dot(left[...], buf[:, cols], preferred_element_type=jnp.float32)
            return c
        lax.fori_loop(0, hid // nt, step, 0)

    def arrive(hop):
        for c in range(chunks):
            for way in range(2):
                k = t - hop if way == 0 else t + hop
                here = k >= 0 if way == 0 else k < tensors
                onward = up_ok if way == 0 else dn_ok
                dest = t + 1 if way == 0 else t - 1

                @pl.when(jnp.logical_and(hop > 0, here))
                def _():
                    z_copy(way, hop, c, k, t).wait_recv()

                @pl.when(jnp.logical_and(here, onward))
                def _():
                    z_copy(way, hop + 1, c, k, dest).start()

    def process(k):
        w_copy(weight_a, wbuf_a, 0, k).start()
        pt = min(fs, 256)

        def pack(n, c):
            cols = pl.ds(pl.multiple_of(n * pt, pt), pt)
            outbox[k, :, cols] = jnp.dot(
                dispatch[...], feats[k, :, cols], preferred_element_type=jnp.float32
            ).astype(jnp.bfloat16)
            return c

        lax.fori_loop(0, fs // pt, pack, 0)
        own_copy(k).start()

        def send(r, c):
            m_copy(k, lax.rem(s + r, sections), s).start()
            return c

        lax.fori_loop(1, sections, send, 0)

    def actor(k):
        gain = gain_a[k]

        def write(rr, v):
            work[rr, :] = v

        scale_rows(lambda rr: feats[k, rr, :], write, sq_a, gain, tok)
        w_copy(weight_a, wbuf_a, 0, k).wait()
        accumulate(acc_a, work, wbuf_a)

    def member(k):
        w_copy(weight_m, wbuf_m, 1, k).start()
        own_copy(k).wait()

        def take(r, c):
            m_copy(k, s, lax.rem(s + r, sections)).wait_recv()
            return c

        lax.fori_loop(1, sections, take, 0)
        gain = gain_m[k]

        def write(rr, v):
            inbox[k, rr, :] = v

        scale_rows(lambda rr: inbox[k, rr, :], write, sq_m, gain, slots)
        w_copy(weight_m, wbuf_m, 1, k).wait()
        accumulate(acc_m, inbox.at[k], wbuf_m)

    def hop_body(hop, c):
        @pl.when(hop < tensors)
        def _():
            arrive(hop)

        def inner(way, c):
            k = jnp.where(way == 0, t - hop, t + hop)
            fine = jnp.logical_and(jnp.logical_and(k >= 0, k < tensors), jnp.logical_or(hop > 0, way == 0))
            fine = jnp.logical_and(fine, hop < tensors)

            @pl.when(fine)
            def _():
                process(k)
                actor(k)
            return c

        lax.fori_loop(0, 2, inner, 0)

        @pl.when(hop == tensors - 1)
        def _():
            pltpu.make_async_copy(b_src(s), blocks.at[s], b_recv.at[s]).start()

            def send(r, c):
                b_copy(lax.rem(s + r, sections), s).start()
                return c

            lax.fori_loop(1, sections, send, 0)

        def inner_m(way, c):
            k = jnp.where(way == 0, t - (hop - 1), t + (hop - 1))
            fine = jnp.logical_and(jnp.logical_and(k >= 0, k < tensors), jnp.logical_or(hop > 1, way == 0))
            fine = jnp.logical_and(fine, hop > 0)

            @pl.when(fine)
            def _():
                member(k)
            return c

        lax.fori_loop(0, 2, inner_m, 0)
        return c

    lax.fori_loop(0, tensors + 1, hop_body, 0)

    pltpu.make_async_copy(b_src(s), blocks.at[s], b_recv.at[s]).wait()

    def finish(r, c):
        other = lax.rem(s + r, sections)
        b_copy(s, other).wait_recv()
        b_copy(other, s).wait_send()

        def sent(k, c):
            m_copy(k, other, s).wait_send()
            return c

        return lax.fori_loop(0, tensors, sent, c)

    lax.fori_loop(1, sections, finish, 0)

    def drain(hop, c):
        for cc in range(chunks):
            @pl.when(jnp.logical_and(t - hop >= 0, up_ok))
            def _():
                z_copy(0, hop + 1, cc, t - hop, t + 1).wait_send()

            @pl.when(jnp.logical_and(t + hop < tensors, dn_ok))
            def _():
                z_copy(1, hop + 1, cc, t + hop, t - 1).wait_send()
        return c

    lax.fori_loop(0, tensors, drain, 0)


def body(
    states, lengths, routes, score_gain, score_weight, score_heads,
    actor_gain, actor_weight, actor_heads,
):
    sections = lax.axis_size("section")
    tensors = lax.axis_size("tensor")
    tok, fs = states.shape
    cap = 2 * tok // sections
    slots = sections * cap
    width = score_gain.shape[1]
    hid = actor_weight.shape[1]
    bw = width // sections
    target = routes[:, 0]
    ids = jnp.arange(tok, dtype=jnp.int32)
    same = jnp.logical_and(target[:, None] == target[None, :], ids[:, None] > ids[None, :])
    placed = jnp.sum(same.astype(jnp.int32), axis=1)
    slot_index = target * cap + placed
    hit = jnp.arange(slots, dtype=jnp.int32)[:, None] == slot_index[None, :]
    dispatch = hit.astype(jnp.bfloat16)

    vmem = pl.BlockSpec(memory_space=pltpu.VMEM)
    any_ = pl.BlockSpec(memory_space=pl.ANY)
    f32, bf16 = jnp.float32, jnp.bfloat16
    acc_m, acc_a, sq_m, sq_a, blocks = pl.pallas_call(
        functools.partial(exchange, sections, tensors, cap),
        out_shape=(
            jax.ShapeDtypeStruct((slots, hid), f32),
            jax.ShapeDtypeStruct((tok, hid), f32),
            jax.ShapeDtypeStruct((slots, 128), f32),
            jax.ShapeDtypeStruct((tok, 128), f32),
            jax.ShapeDtypeStruct((sections, tok, bw), bf16),
        ),
        in_specs=[any_, vmem, vmem, vmem, any_, any_],
        out_specs=(vmem, vmem, vmem, vmem, any_),
        scratch_shapes=[
            pltpu.VMEM((tensors, tok, fs), bf16),
            pltpu.VMEM((tensors, slots, fs), bf16),
            pltpu.VMEM((tensors, slots, fs), bf16),
            pltpu.VMEM((tok, fs), bf16),
            pltpu.VMEM((fs, hid), bf16),
            pltpu.VMEM((fs, hid), bf16),
            pltpu.SemaphoreType.DMA((2, tensors + 1, 2)),
            pltpu.SemaphoreType.DMA((2, tensors + 1, 2)),
            pltpu.SemaphoreType.DMA((tensors, sections)),
            pltpu.SemaphoreType.DMA((tensors, sections)),
            pltpu.SemaphoreType.DMA((sections,)),
            pltpu.SemaphoreType.DMA((sections,)),
            pltpu.SemaphoreType.DMA((1,)),
            pltpu.SemaphoreType.DMA((2,)),
        ],
        compiler_params=pltpu.CompilerParams(
            collective_id=0, has_side_effects=True, vmem_limit_bytes=67043328
        ),
    )(
        states, dispatch, score_gain[0].reshape(tensors, 1, fs),
        actor_gain.reshape(tensors, 1, fs), score_weight[0], actor_weight,
    )

    actor_scale = lax.rsqrt(jnp.sum(sq_a, axis=1) / width + epsilon)
    actor_pre = acc_a * actor_scale[:, None]
    sigmoid_pre = jax.nn.sigmoid(actor_pre)
    silu_slope = sigmoid_pre * (1.0 + actor_pre * (1.0 - sigmoid_pre))
    early = (actor_scale[:, None] * actor_heads[None, :] * silu_slope).astype(bf16)
    every_early = lax.all_gather(early, "section", axis=0, tiled=True)
    shift_part = jnp.sum(actor_pre * sigmoid_pre * actor_heads[None, :], axis=1)

    member_scale = lax.rsqrt(jnp.sum(sq_m, axis=1) / width + epsilon)
    preact = acc_m * member_scale[:, None]
    act = jax.nn.silu(preact)
    heads = score_heads[0]
    parts = jnp.stack(
        [jnp.sum(act * heads[:, 0][None, :], axis=1), jnp.sum(act * heads[:, 1][None, :], axis=1)]
    )
    scores, log_shift = lax.psum((parts, shift_part), "tensor")
    returned = lax.all_to_all(
        scores.reshape(2, sections, cap), "section", split_axis=1, concat_axis=1, tiled=True
    ).reshape(2, slots)
    values = jnp.sum(jnp.where(hit, returned[0][:, None], 0.0), axis=0)
    rewards = jnp.sum(jnp.where(hit, returned[1][:, None], 0.0), axis=0)

    ends = jnp.sum(
        jnp.where(jnp.arange(lengths.shape[1])[:, None] <= jnp.arange(lengths.shape[1])[None, :],
                  lengths[0][:, None], 0), axis=0) - 1
    last = jnp.any(ids[:, None] == ends[None, :], axis=1)
    response = jnp.sum((ids[:, None] > ends[None, :]).astype(jnp.int32), axis=1)
    gap = ids[None, :] - ids[:, None]
    linked = jnp.logical_and(gap >= 0, response[:, None] == response[None, :])
    decay = jnp.where(linked, jnp.exp(gap.astype(f32) * jnp.log(f32(trace_decay))), 0.0)
    following = jnp.concatenate([values[1:], jnp.zeros_like(values[:1])])
    delta = jnp.where(last, rewards, following) - values
    raw = jnp.sum(decay * delta[None, :], axis=1)

    both = lax.all_gather(jnp.stack([raw, log_shift]), "section", axis=0)
    raw_all = both[:, 0].reshape(-1)
    shift_all = both[:, 1].reshape(-1)
    total = tok * sections
    center = jnp.sum(raw_all) / total
    spread = jnp.sum(raw_all * raw_all) / total - center * center
    inv = lax.rsqrt(spread + epsilon)
    advantages = (raw - center) * inv
    ratios = jnp.exp(shift_all)
    slope = penalty * (ratios - 1.0) - ratios * ((raw_all - center) * inv)

    gain_own = lax.dynamic_slice(actor_gain, (lax.axis_index("section") * bw,), (bw,))
    left = (blocks.reshape(total, bw).astype(f32) * gain_own[None, :]).astype(bf16)
    right = (every_early.astype(f32) * slope[:, None]).astype(bf16)
    actor_grad = lax.dot_general(
        left, right, (((0,), (0,)), ((), ())), preferred_element_type=f32
    )
    return (scores, advantages, actor_grad)


def solution(mesh):
    in_specs = (
        P("section", "tensor"),
        P("section", None),
        P("section", None),
        P("section", None),
        P("section", None, "tensor"),
        P("section", "tensor", None),
        P(),
        P(None, "tensor"),
        P("tensor"),
    )
    out_specs = (P(None, "section"), P("section"), P("section", "tensor"))
    return jax.shard_map(body, mesh=mesh, in_specs=in_specs, out_specs=out_specs, check_vma=False)
```

time: 718 us -> 380 us (0.53)
  waiting for transfers between devices: 361 us -> 14.5 us
  Pallas kernels: 0 us -> 285 us
  blocking collectives: 215 us -> 27.2 us
  matrix products: 60.8 us -> 15.5 us
  local copies, waits for them, and re-layouts: 35 us -> 1.38 us
    all_gather x3 -> x1, waiting for transfers between devices: 357 us -> 10.8 us  [body(): every_early = lax.all_gather(early, 'section', axis=0, tiled=True)]
    pallas_call x0 -> x1, Pallas kernels: none -> 285 us  [body(): pl.pallas_call(functools.partial(exchange, sections, tensors, cap), out_s...]
    all_to_all x2 -> x0, blocking collectives: 187 us -> none  [the longest x1 132 us: body(): lax.all_to_all(gained, 'section', split_axis=1, concat_axis=0, tiled=True)]
    dot_general x6 -> x1, matrix products: 60.8 us -> 15.5 us  [body(): lax.dot_general(left, right, (((0,), (0,)), ((), ())), preferred_element_...]
    all_to_all x2 -> x0, local copies, waits for them, and re-layouts: 11.7 us -> none  [the longest x1 11.5 us: body(): lax.all_to_all(gained, 'section', split_axis=1, concat_axis=0, tiled=True)]
    slice x59 -> x3, local copies, waits for them, and re-layouts: 11.5 us -> 0.09 us  [the longest x1 0.07 us: body(): following = jnp.concatenate([values[1:], jnp.zeros_like(values[:1])])]
    psum x2 -> x1, blocking collectives: 28.9 us -> 18.4 us  [body(): scores, log_shift = lax.psum((parts, shift_part), 'tensor')]
    all_gather x0 -> x1, blocking collectives: none -> 8.77 us  [body(): both = lax.all_gather(jnp.stack([raw, log_shift]), 'section', axis=0)]
  transfers between devices with their start and end apart: 4 -> 2, of which waited for: 3 -> 2; matrix products, arithmetic and copies ran while one was open for 5% -> 2% of each run, Pallas kernels for 0% -> 0%
where the time goes in v1:
time: 380 us; the launch traced here: 379 us
  Pallas kernels  285 us (75%)
  blocking collectives  27.2 us (7%)
  between operations  16.8 us (4%)
  matrix products  15.5 us (4%)
  other arithmetic  15 us (4%)
  waiting for transfers between devices  14.5 us (4%)
    pallas_call x1, Pallas kernels, body(): pl.pallas_call(functools.partial(exchange, sections, tensors, cap), out_s...  285 us
    psum x1, blocking collectives, body(): scores, log_shift = lax.psum((parts, shift_part), 'tensor')  18.4 us
    dot_general x1, matrix products, body(): lax.dot_general(left, right, (((0,), (0,)), ((), ())), preferred_element_...  15.5 us
    all_gather x1, waiting for transfers between devices, body(): every_early = lax.all_gather(early, 'section', axis=0, tiled=True)  10.8 us
    all_gather x1, blocking collectives, body(): both = lax.all_gather(jnp.stack([raw, log_shift]), 'section', axis=0)  8.77 us
  transfers between devices with their start and end apart: 2, of which 2 were waited for; matrix products, arithmetic and copies ran while one was open for 2% of the time, Pallas kernels for 0%

profile of v1, /device:TPU:0, one launch (start us, length us, event | category | flops | bytes accessed | tf_op | source)
XLA Modules:
  0.0 379.1 jit_solution(15003905824556605542)
XLA Ops:
  7.2 1.0 convert_reduce_fusion
  8.2 0.7 multiply_add_fusion
  8.9 0.6 copy-done.1
  9.5 1.4 fusion.5.dispatch
  10.9 285.4 %shard_map.112 = (f32[1024,1024]{1,0:T(8,128)}, f32[512,1024]{1,0:T(8,128)}, f32[1024,128]{1,0:T(8,128)}, f32[512,128]{1,0:T(8,128)}, bf16[8,512,1024]{2,1,0:T(8,128)(2,1)}) custom-call(bf16[512,2048]{1,0:T(8,128)(2,1)} %states.1, bf16[1024,512]{1,0:T(8,128)(2,1)} %fusion.5.dispatch, f32[4,1,2048]{2,1,0:T(1,128)} %bitcast.25, f32[4,1,2048]{2,1,0:T(1,128)} %bitcast.24, ...), custom_call_target="tpu_custom_call" | custom-call | tf_op jit(solution)/shard_map/pallas_call | solution.py:279
  296.3 1.1 reduce_sum.126
  297.5 3.7 multiply_convert_fusion.2
  301.2 0.2 reduce_sum.118
  301.5 3.8 multiply_reduce_fusion.1
  305.3 18.4 %all-reduce = (f32[2,1024]{1,0:T(2,128)}, f32[1,512]{1,0:T(1,128)S(1)}) all-reduce(f32[2,1024]{1,0:T(2,128)S(1)} %pad_maximum_fusion, f32[1,512]{1,0:T(1,128)S(1)} %bitcast.35), channel_id=1, replica_groups=mesh['section'=8,'tensor'=4] {'tensor'}, use_global_device_ids=true, to_apply=%region_4.5 | all-reduce | flops 2560 | bytes 20480 | tf_op jit(solution)/shard_map/psum | solution.py:329
  323.7 3.3 all-to-all-start
  327.0 0.1 select_reduce_fusion.2
  327.1 0.1 fusion.9
  327.2 0.1 convert_reduce_fusion.1
  327.3 0.7 dynamic_slice.3
  328.0 3.7 all-to-all-done
  331.7 0.4 select_reduce_fusion.1
  332.3 0.4 multiply_reduce_fusion.3
  332.6 8.8 %all-gather.1 = f32[8,2,512]{2,1,0:T(2,128)S(1)} all-gather(f32[1,2,512]{2,1,0:T(2,128)S(1)} %maximum_bitcast_fusion), channel_id=2, replica_groups=mesh['section'=8,'tensor'=4] {'section'}, dimensions={0}, use_global_device_ids=true | all-gather | bytes 36864 | tf_op jit(solution)/shard_map/all_gather | solution.py:348
  341.4 0.6 fusion.11
  344.0 0.6 multiply_reduce_fusion.4
  345.3 0.6 subtract_multiply_fusion
  345.9 10.8 %all-gather.4.cloned.1.call-done = bf16[4096,1024]{1,0:T(8,128)(2,1)} async-done(((bf16[512,1024]{1,0:T(8,128)(2,1)}), bf16[4096,1024]{1,0:T(8,128)(2,1)}) %all-gather.4.cloned.1.call-update) | async-done | bytes 8388624 | tf_op jit(solution)/shard_map/all_gather | solution.py:319
  356.8 15.5 %fusion.1 = f32[1024,1024]{1,0:T(8,128)} fusion(bf16[4096,1024]{1,0:T(8,128)(2,1)} %all-gather.4.cloned.1.call-done, bf16[4096,1024]{1,0:T(8,128)(2,1)} %bitcast.38, f32[4096]{0:T(1024)S(1)} %bitcast.32, f32[1024]{0:T(1024)S(1)} %dynamic_slice.3), kind=kOutput, calls=%fused_computation.3 | convolution fusion | flops 8615100416 | bytes 20992000 | tf_op jit(solution)/shard_map/dot_general | solution.py:362
  (22 shorter events, 0.3 us)
Async XLA Ops:
  7.2 349.6 %all-gather.4.cloned.1.call-start = ((), (), s32[]{:S(2)}) async-start(), calls=%async_computation.1 | async-start | bytes 9437184 | tf_op jit(solution)/shard_map/all_gather | solution.py:319
  8.9 0.6 copy-start.1
  296.3 4.9 %copy-start = (f32[1024,128]{1,0:T(8,128)S(1)}, f32[1024,128]{1,0:T(8,128)}, u32[]{:S(2)}) copy-start(f32[1024,128]{1,0:T(8,128)} %get-tuple-element.9) | copy-start | bytes 1572868
  296.3 5.2 %copy-start.3 = (f32[1,1024,2]{1,2,0:T(2,128)S(1)}, f32[1,1024,2]{1,2,0:T(2,128)}, u32[]{:S(2)}) copy-start(f32[1,1024,2]{1,2,0:T(2,128)} %param.14) | copy-start | bytes 24580
  297.5 29.5 %copy-start.4 = (s32[1,16]{1,0:T(1,128)S(1)}, s32[1,16]{1,0:T(1,128)}, u32[]{:S(2)}) copy-start(s32[1,16]{1,0:T(1,128)} %param.10) | copy-start | bytes 196
  297.5 34.2 %copy-start.2 = (s32[512]{0:T(512)S(1)}, s32[512]{0:T(512)}, u32[]{:S(2)}) copy-start(s32[512]{0:T(512)} %copy-done.1) | copy-start | bytes 6148
  323.7 8.0 %all-to-all-start = ((f32[2,8,128]{2,0,1:T(2,128)}), f32[2,8,128]{2,0,1:T(2,128)S(1)}, u32[]{:S(2)}, u32[]{:S(2)}) async-start(f32[2,8,128]{2,0,1:T(2,128)} %bitcast.10), calls=%async_computation | async-start | bytes 16384 | tf_op jit(solution)/shard_map/all_to_all | solution.py:330
Sparse Core Ops, SparseCore 0:
  301.3 55.4 all-gather.3

commit v2 on v1

--- a/solution.py
+++ b/solution.py
@@ -14,10 +14,11 @@
 
 def exchange(
     sections, tensors, cap,
-    states, dispatch, gain_m, gain_a, weight_m, weight_a,
-    acc_m, acc_a, sq_m, sq_a, blocks,
-    feats, outbox, inbox, work, wbuf_m, wbuf_a,
+    states, dispatch, gain_m, gain_a, weight_m, weight_a, heads_m, heads_a, final,
+    scores, pairs, blocks, hidden,
+    acc_m, acc_a, sq_m, sq_a, lanes, part, part_a, back, early, feats, outbox, inbox, work, wbuf_m, wbuf_a,
     z_send, z_recv, m_send, m_recv, b_send, b_recv, loc_sem, w_sem,
+    t_send, t_recv, u_send, u_recv, r_send, r_recv, p_send, p_recv, g_send, g_recv, g_pass,
 ):
     s = lax.axis_index("section")
     t = lax.axis_index("tensor")
@@ -43,16 +44,12 @@
 
     lax.fori_loop(1, sections, greet, 0)
 
-    @pl.when(up_ok)
-    def _():
-        pl.semaphore_signal(barrier, inc=1, device_id=(s, t + 1), device_id_type=MESH)
-
-    @pl.when(dn_ok)
-    def _():
-        pl.semaphore_signal(barrier, inc=1, device_id=(s, t - 1), device_id_type=MESH)
-
-    peers = sections - 1 + jnp.where(up_ok, 1, 0) + jnp.where(dn_ok, 1, 0)
-    pl.semaphore_wait(barrier, peers)
+    def greet_z(r, c):
+        pl.semaphore_signal(barrier, inc=1, device_id=(s, lax.rem(t + r, tensors)), device_id_type=MESH)
+        return c
+
+    lax.fori_loop(1, tensors, greet_z, 0)
+    pl.semaphore_wait(barrier, sections - 1 + tensors - 1)
 
     acc_m[...] = jnp.zeros_like(acc_m)
     acc_a[...] = jnp.zeros_like(acc_a)
@@ -181,6 +178,220 @@
         w_copy(weight_m, wbuf_m, 1, k).wait()
         accumulate(acc_m, inbox.at[k], wbuf_m)
 
+    partner = s + 1 - 2 * lax.rem(s, 2)
+    chips = sections // 2
+    width = fs * tensors
+
+    def send_block(r, c):
+        b_copy(lax.rem(s + r, sections), s).start()
+        return c
+
+    def g_copy(dest, src):
+        return pltpu.make_async_remote_copy(
+            src_ref=early, dst_ref=hidden.at[src],
+            send_sem=g_send.at[dest], recv_sem=g_recv.at[src],
+            device_id=(dest, t), device_id_type=MESH,
+        )
+
+    def g_relay(src):
+        return pltpu.make_async_remote_copy(
+            src_ref=hidden.at[src], dst_ref=hidden.at[src],
+            send_sem=g_pass.at[src], recv_sem=g_recv.at[src],
+            device_id=(partner, t), device_id_type=MESH,
+        )
+
+    def own_hidden():
+        return pltpu.make_async_copy(early, hidden.at[s], g_recv.at[s])
+
+    def t_copy(dest, src):
+        return pltpu.make_async_remote_copy(
+            src_ref=part.at[src], dst_ref=part.at[src],
+            send_sem=t_send.at[dest], recv_sem=t_recv.at[src],
+            device_id=(s, dest), device_id_type=MESH,
+        )
+
+    def u_copy(dest, src):
+        return pltpu.make_async_remote_copy(
+            src_ref=part_a.at[src], dst_ref=part_a.at[src],
+            send_sem=u_send.at[dest], recv_sem=u_recv.at[src],
+            device_id=(s, dest), device_id_type=MESH,
+        )
+
+    def r_copy(dest, src):
+        return pltpu.make_async_remote_copy(
+            src_ref=scores.at[dest], dst_ref=back.at[src],
+            send_sem=r_send.at[dest], recv_sem=r_recv.at[src],
+            device_id=(dest, t), device_id_type=MESH,
+        )
+
+    def p_copy(dest, src):
+        return pltpu.make_async_remote_copy(
+            src_ref=pairs.at[src], dst_ref=pairs.at[src],
+            send_sem=p_send.at[dest], recv_sem=p_recv.at[src],
+            device_id=(dest, t), device_id_type=MESH,
+        )
+
+    def across(x):
+        return lax.dot_general(
+            jnp.ones((8, 128), jnp.float32), x, (((1,), (1,)), ((), ())),
+            precision=lax.Precision.HIGHEST, preferred_element_type=jnp.float32,
+        )
+
+    def fold(x):
+        total = x[:, 0:128]
+        for j in range(1, hid // 128):
+            total = total + x[:, j * 128:(j + 1) * 128]
+        return total
+
+    def hidden_step():
+        def step(i, c):
+            rr = pl.ds(pl.multiple_of(i * rb, rb), rb)
+            scale = lax.rsqrt(jnp.sum(sq_a[rr, :], axis=1, keepdims=True) / width + epsilon)
+            pre = acc_a[rr, :] * scale
+            sig = 1.0 / (1.0 + jnp.exp(-pre))
+            row = heads_a[...]
+            early[rr, :] = (scale * row * (sig * (1.0 + pre * (1.0 - sig)))).astype(jnp.bfloat16)
+            lanes[0, rr, :] = fold(pre * sig * row)
+            return c
+
+        lax.fori_loop(0, tok // rb, step, 0)
+        part_a[t] = across(lanes[0, 0:tok, :])
+
+        def send_u(r, c):
+            u_copy(lax.rem(t + r, tensors), t).start()
+            return c
+
+        lax.fori_loop(1, tensors, send_u, 0)
+        own_hidden().start()
+        g_copy(partner, s).start()
+
+        def send_g(r, c):
+            g_copy(lax.rem(s + 2 * r, sections), s).start()
+            return c
+
+        lax.fori_loop(1, chips, send_g, 0)
+
+    def score_step():
+        def step(i, c):
+            rr = pl.ds(pl.multiple_of(i * rb, rb), rb)
+            scale = lax.rsqrt(jnp.sum(sq_m[rr, :], axis=1, keepdims=True) / width + epsilon)
+            pre = acc_m[rr, :] * scale
+            act = pre * (1.0 / (1.0 + jnp.exp(-pre)))
+            lanes[0, rr, :] = fold(act * heads_m[0:1, :])
+            lanes[1, rr, :] = fold(act * heads_m[1:2, :])
+            return c
+
+        lax.fori_loop(0, slots // rb, step, 0)
+        first = lax.broadcasted_iota(jnp.int32, (8, cap), 0) == 0
+
+        def gather(d, c):
+            rr = pl.ds(pl.multiple_of(d * cap, cap), cap)
+            part[t, d] = jnp.where(first, across(lanes[0, rr, :]), across(lanes[1, rr, :]))
+            return c
+
+        lax.fori_loop(0, sections, gather, 0)
+
+        def send_t(r, c):
+            t_copy(lax.rem(t + r, tensors), t).start()
+            return c
+
+        lax.fori_loop(1, tensors, send_t, 0)
+
+        def take_t(r, c):
+            t_copy(t, lax.rem(t + r, tensors)).wait_recv()
+            u_copy(t, lax.rem(t + r, tensors)).wait_recv()
+            return c
+
+        lax.fori_loop(1, tensors, take_t, 0)
+        scores[...] = lax.fori_loop(1, tensors, lambda k, v: v + part[k], part[0])
+        shift = lax.fori_loop(1, tensors, lambda k, v: v + part_a[k], part_a[0])
+
+        def send_r(r, c):
+            r_copy(lax.rem(s + r, sections), s).start()
+            return c
+
+        lax.fori_loop(1, sections, send_r, 0)
+        back[s] = scores[s]
+        lax.fori_loop(sections - spare, sections, send_block, 0)
+
+        def take_r(r, c):
+            r_copy(s, lax.rem(s + r, sections)).wait_recv()
+            return c
+
+        lax.fori_loop(1, sections, take_r, 0)
+
+        def pick(m, v):
+            x = back[m]
+            hi = x.astype(jnp.bfloat16)
+            rest = x - hi.astype(jnp.float32)
+            mid = rest.astype(jnp.bfloat16)
+            low = (rest - mid.astype(jnp.float32)).astype(jnp.bfloat16)
+            rows = dispatch[pl.ds(pl.multiple_of(m * cap, cap), cap), :]
+            for piece in (low, mid, hi):
+                v = v + jnp.dot(piece, rows, preferred_element_type=jnp.float32)
+            return v
+
+        picked = lax.fori_loop(0, sections, pick, jnp.zeros((8, tok), jnp.float32))
+        values = jnp.broadcast_to(picked[0:1, :], (8, tok))
+        rewards = jnp.broadcast_to(picked[1:2, :], (8, tok))
+        ended = jnp.broadcast_to(final[...], (8, tok)) > 0.5
+        total = jnp.where(ended, rewards, pltpu.roll(values, tok - 1, 1)) - values
+        carry = jnp.where(ended, 0.0, trace_decay)
+        reach = 1
+        while reach < tok:
+            total = total + carry * pltpu.roll(total, tok - reach, 1)
+            carry = carry * pltpu.roll(carry, tok - reach, 1)
+            reach *= 2
+        top = lax.broadcasted_iota(jnp.int32, (8, tok), 0) == 0
+        pairs[s] = jnp.where(top, total, shift)
+
+        def send_p(r, c):
+            p_copy(lax.rem(s + r, sections), s).start()
+            return c
+
+        lax.fori_loop(1, sections, send_p, 0)
+
+        def relay(r, c):
+            src = lax.rem(s + 2 * r, sections)
+            g_copy(s, src).wait_recv()
+            g_relay(src).start()
+            return c
+
+        lax.fori_loop(1, chips, relay, 0)
+        own_hidden().wait()
+
+    def settle():
+        g_copy(s, partner).wait_recv()
+        g_copy(partner, s).wait_send()
+
+        def done_g(r, c):
+            other = lax.rem(s + 2 * r, sections)
+            g_copy(other, s).wait_send()
+            g_relay(other).wait_send()
+            g_copy(s, lax.rem(partner + 2 * r, sections)).wait_recv()
+            return c
+
+        lax.fori_loop(1, chips, done_g, 0)
+
+        def done_z(r, c):
+            other = lax.rem(t + r, tensors)
+            t_copy(other, t).wait_send()
+            u_copy(other, t).wait_send()
+            return c
+
+        lax.fori_loop(1, tensors, done_z, 0)
+
+        def done_s(r, c):
+            other = lax.rem(s + r, sections)
+            r_copy(other, s).wait_send()
+            p_copy(other, s).wait_send()
+            p_copy(s, other).wait_recv()
+            return c
+
+        lax.fori_loop(1, sections, done_s, 0)
+
+    spare = max(1, 3 * sections // 8)
+
     def hop_body(hop, c):
         @pl.when(hop < tensors)
         def _():
@@ -201,13 +412,9 @@
 
         @pl.when(hop == tensors - 1)
         def _():
+            hidden_step()
             pltpu.make_async_copy(b_src(s), blocks.at[s], b_recv.at[s]).start()
-
-            def send(r, c):
-                b_copy(lax.rem(s + r, sections), s).start()
-                return c
-
-            lax.fori_loop(1, sections, send, 0)
+            lax.fori_loop(1, sections - spare, send_block, 0)
 
         def inner_m(way, c):
             k = jnp.where(way == 0, t - (hop - 1), t + (hop - 1))
@@ -223,6 +430,8 @@
         return c
 
     lax.fori_loop(0, tensors + 1, hop_body, 0)
+    score_step()
+    settle()
 
     pltpu.make_async_copy(b_src(s), blocks.at[s], b_recv.at[s]).wait()
 
@@ -272,22 +481,34 @@
     slot_index = target * cap + placed
     hit = jnp.arange(slots, dtype=jnp.int32)[:, None] == slot_index[None, :]
     dispatch = hit.astype(jnp.bfloat16)
+    count = lengths.shape[1]
+    order = jnp.arange(count, dtype=jnp.int32)
+    ends = jnp.sum(jnp.where(order[:, None] <= order[None, :], lengths[0][:, None], 0), axis=0) - 1
+    last = jnp.any(ends[:, None] == ids[None, :], axis=0)
 
     vmem = pl.BlockSpec(memory_space=pltpu.VMEM)
     any_ = pl.BlockSpec(memory_space=pl.ANY)
     f32, bf16 = jnp.float32, jnp.bfloat16
-    acc_m, acc_a, sq_m, sq_a, blocks = pl.pallas_call(
+    scores, pairs, blocks, hidden = pl.pallas_call(
         functools.partial(exchange, sections, tensors, cap),
         out_shape=(
-            jax.ShapeDtypeStruct((slots, hid), f32),
-            jax.ShapeDtypeStruct((tok, hid), f32),
-            jax.ShapeDtypeStruct((slots, 128), f32),
-            jax.ShapeDtypeStruct((tok, 128), f32),
+            jax.ShapeDtypeStruct((sections, 8, cap), f32),
+            jax.ShapeDtypeStruct((sections, 8, tok), f32),
             jax.ShapeDtypeStruct((sections, tok, bw), bf16),
+            jax.ShapeDtypeStruct((sections, tok, hid), bf16),
         ),
-        in_specs=[any_, vmem, vmem, vmem, any_, any_],
-        out_specs=(vmem, vmem, vmem, vmem, any_),
+        in_specs=[any_, vmem, vmem, vmem, any_, any_, vmem, vmem, vmem],
+        out_specs=(vmem, vmem, any_, any_),
         scratch_shapes=[
+            pltpu.VMEM((slots, hid), f32),
+            pltpu.VMEM((tok, hid), f32),
+            pltpu.VMEM((slots, 128), f32),
+            pltpu.VMEM((tok, 128), f32),
+            pltpu.VMEM((2, max(slots, tok), 128), f32),
+            pltpu.VMEM((tensors, sections, 8, cap), f32),
+            pltpu.VMEM((tensors, 8, tok), f32),
+            pltpu.VMEM((sections, 8, cap), f32),
+            pltpu.VMEM((tok, hid), bf16),
             pltpu.VMEM((tensors, tok, fs), bf16),
             pltpu.VMEM((tensors, slots, fs), bf16),
             pltpu.VMEM((tensors, slots, fs), bf16),
@@ -302,6 +523,17 @@
             pltpu.SemaphoreType.DMA((sections,)),
             pltpu.SemaphoreType.DMA((1,)),
             pltpu.SemaphoreType.DMA((2,)),
+            pltpu.SemaphoreType.DMA((tensors,)),
+            pltpu.SemaphoreType.DMA((tensors,)),
+            pltpu.SemaphoreType.DMA((tensors,)),
+            pltpu.SemaphoreType.DMA((tensors,)),
+            pltpu.SemaphoreType.DMA((sections,)),
+            pltpu.SemaphoreType.DMA((sections,)),
+            pltpu.SemaphoreType.DMA((sections,)),
+            pltpu.SemaphoreType.DMA((sections,)),
+            pltpu.SemaphoreType.DMA((sections,)),
+            pltpu.SemaphoreType.DMA((sections,)),
+            pltpu.SemaphoreType.DMA((sections,)),
         ],
         compiler_params=pltpu.CompilerParams(
             collective_id=0, has_side_effects=True, vmem_limit_bytes=67043328
@@ -309,45 +541,12 @@
     )(
         states, dispatch, score_gain[0].reshape(tensors, 1, fs),
         actor_gain.reshape(tensors, 1, fs), score_weight[0], actor_weight,
+        jnp.transpose(score_heads[0]), actor_heads[None, :], last.astype(f32)[None, :],
     )
 
-    actor_scale = lax.rsqrt(jnp.sum(sq_a, axis=1) / width + epsilon)
-    actor_pre = acc_a * actor_scale[:, None]
-    sigmoid_pre = jax.nn.sigmoid(actor_pre)
-    silu_slope = sigmoid_pre * (1.0 + actor_pre * (1.0 - sigmoid_pre))
-    early = (actor_scale[:, None] * actor_heads[None, :] * silu_slope).astype(bf16)
-    every_early = lax.all_gather(early, "section", axis=0, tiled=True)
-    shift_part = jnp.sum(actor_pre * sigmoid_pre * actor_heads[None, :], axis=1)
-
-    member_scale = lax.rsqrt(jnp.sum(sq_m, axis=1) / width + epsilon)
-    preact = acc_m * member_scale[:, None]
-    act = jax.nn.silu(preact)
-    heads = score_heads[0]
-    parts = jnp.stack(
-        [jnp.sum(act * heads[:, 0][None, :], axis=1), jnp.sum(act * heads[:, 1][None, :], axis=1)]
-    )
-    scores, log_shift = lax.psum((parts, shift_part), "tensor")
-    returned = lax.all_to_all(
-        scores.reshape(2, sections, cap), "section", split_axis=1, concat_axis=1, tiled=True
-    ).reshape(2, slots)
-    values = jnp.sum(jnp.where(hit, returned[0][:, None], 0.0), axis=0)
-    rewards = jnp.sum(jnp.where(hit, returned[1][:, None], 0.0), axis=0)
-
-    ends = jnp.sum(
-        jnp.where(jnp.arange(lengths.shape[1])[:, None] <= jnp.arange(lengths.shape[1])[None, :],
-                  lengths[0][:, None], 0), axis=0) - 1
-    last = jnp.any(ids[:, None] == ends[None, :], axis=1)
-    response = jnp.sum((ids[:, None] > ends[None, :]).astype(jnp.int32), axis=1)
-    gap = ids[None, :] - ids[:, None]
-    linked = jnp.logical_and(gap >= 0, response[:, None] == response[None, :])
-    decay = jnp.where(linked, jnp.exp(gap.astype(f32) * jnp.log(f32(trace_decay))), 0.0)
-    following = jnp.concatenate([values[1:], jnp.zeros_like(values[:1])])
-    delta = jnp.where(last, rewards, following) - values
-    raw = jnp.sum(decay * delta[None, :], axis=1)
-
-    both = lax.all_gather(jnp.stack([raw, log_shift]), "section", axis=0)
-    raw_all = both[:, 0].reshape(-1)
-    shift_all = both[:, 1].reshape(-1)
+    raw_all = pairs[:, 0].reshape(-1)
+    shift_all = pairs[:, 1].reshape(-1)
+    raw = lax.dynamic_index_in_dim(pairs, lax.axis_index("section"), 0, keepdims=False)[0]
     total = tok * sections
     center = jnp.sum(raw_all) / total
     spread = jnp.sum(raw_all * raw_all) / total - center * center
@@ -358,11 +557,12 @@
 
     gain_own = lax.dynamic_slice(actor_gain, (lax.axis_index("section") * bw,), (bw,))
     left = (blocks.reshape(total, bw).astype(f32) * gain_own[None, :]).astype(bf16)
-    right = (every_early.astype(f32) * slope[:, None]).astype(bf16)
+    right = (hidden.reshape(total, hid).astype(f32) * slope[:, None]).astype(bf16)
     actor_grad = lax.dot_general(
         left, right, (((0,), (0,)), ((), ())), preferred_element_type=f32
     )
-    return (scores, advantages, actor_grad)
+    packed_scores = jnp.transpose(scores[:, :2], (1, 0, 2)).reshape(2, slots)
+    return (packed_scores, advantages, actor_grad)
 
 
 def solution(mesh):

time: 380 us -> 368 us (0.968)
  Pallas kernels: 285 us -> 337 us
  blocking collectives: 27.2 us -> 0 us
  waiting for transfers between devices: 14.5 us -> 0 us
  between operations: 16.8 us -> 3.29 us
  other arithmetic: 15 us -> 8.38 us
    pallas_call x1, Pallas kernels: 285 us -> 337 us  [body(): pl.pallas_call(functools.partial(exchange, sections, tensors, cap), out_s...]
    psum x1 -> x0, blocking collectives: 18.4 us -> none  [body(): scores, log_shift = lax.psum((parts, shift_part), 'tensor')]
    all_gather x1 -> x0, waiting for transfers between devices: 10.8 us -> none  [body(): every_early = lax.all_gather(early, 'section', axis=0, tiled=True)]
    all_gather x1 -> x0, blocking collectives: 8.77 us -> none  [body(): both = lax.all_gather(jnp.stack([raw, log_shift]), 'section', axis=0)]
    reduce_sum x8 -> x2, other arithmetic: 6.74 us -> 2.29 us  [the longest x1 1.55 us: body(): center = jnp.sum(raw_all) / total]
  transfers between devices with their start and end apart: 2 -> 0, of which waited for: 2 -> 0; matrix products, arithmetic and copies ran while one was open for 2% -> 0% of each run, Pallas kernels for 0% -> 0%
where the time goes in v2:
time: 368 us; the launch traced here: 367 us
  Pallas kernels  337 us (92%)
  matrix products  15.5 us (4%)
  other arithmetic  8.38 us (2%)
    pallas_call x1, Pallas kernels, body(): pl.pallas_call(functools.partial(exchange, sections, tensors, cap), out_s...  337 us
    dot_general x1, matrix products, body(): lax.dot_general(left, right, (((0,), (0,)), ((), ())), preferred_element_...  15.5 us

profile of v2, /device:TPU:0, one launch (start us, length us, event | category | flops | bytes accessed | tf_op | source)
XLA Modules:
  0.0 366.9 jit_solution(12818817595168157140)
XLA Ops:
  0.6 0.7 select_reduce_fusion
  1.4 0.1 fusion.6
  1.5 0.6 convert_element_type.43
  2.1 1.0 convert_reduce_fusion
  3.1 0.7 multiply_add_fusion
  3.8 1.3 dynamic_slice.8
  5.0 1.4 fusion.4.dispatch
  6.4 337.0 %shard_map.112 = (f32[8,8,128]{2,1,0:T(8,128)}, f32[8,8,512]{2,1,0:T(8,128)}, bf16[8,512,1024]{2,1,0:T(8,128)(2,1)}, bf16[8,512,1024]{2,1,0:T(8,128)(2,1)}) custom-call(bf16[512,2048]{1,0:T(8,128)(2,1)} %states.1, bf16[1024,512]{1,0:T(8,128)(2,1)} %fusion.4.dispatch, f32[4,1,2048]{2,1,0:T(1,128)} %bitcast.22, f32[4,1,2048]{2,1,0:T(1,128)} %bitcast.21, ...), custom_call_target="tpu_custom_call" | custom-call | tf_op jit(solution)/shard_map/pallas_call | solution.py:492
  343.5 1.4 slice_bitcast_fusion
  344.8 1.5 slice_reduce_fusion
  349.0 1.3 fusion.7
  350.3 1.0 multiply_subtract_fusion
  351.3 15.5 %fusion.3 = f32[1024,1024]{1,0:T(8,128)} fusion(bf16[8,512,1024]{2,1,0:T(8,128)(2,1)} %get-tuple-element.10, f32[8,512]{1,0:T(8,128)S(1)} %bitcast.25, bf16[8,512,1024]{2,1,0:T(8,128)(2,1)} %get-tuple-element.9, f32[1024]{0:T(1024)} %dynamic_slice.8), kind=kOutput, calls=%fused_computation.5 | convolution fusion | flops 8615100416 | bytes 20992000 | tf_op jit(solution)/shard_map/dot_general | solution.py:561
  (2 shorter events, 0.0 us)

commit v3 on v2

--- a/solution.py
+++ b/solution.py
@@ -19,6 +19,7 @@
     acc_m, acc_a, sq_m, sq_a, lanes, part, part_a, back, early, feats, outbox, inbox, work, wbuf_m, wbuf_a,
     z_send, z_recv, m_send, m_recv, b_send, b_recv, loc_sem, w_sem,
     t_send, t_recv, u_send, u_recv, r_send, r_recv, p_send, p_recv, g_send, g_recv, g_pass,
+    q_send, q_recv, y_send, y_recv,
 ):
     s = lax.axis_index("section")
     t = lax.axis_index("tensor")
@@ -73,15 +74,56 @@
             device_id=(dest, t), device_id_type=MESH,
         )
 
-    def b_src(dest):
-        return feats.at[dest // bps, :, pl.ds(pl.multiple_of(lax.rem(dest, bps) * bw, bw), bw)]
+    share = max(16, (3 * tok // 4) // tensors // 16 * 16)
+    zr = share * tensors
+
+    def b_src(dest, row, count):
+        return feats.at[dest // bps, pl.ds(row, count), pl.ds(pl.multiple_of(lax.rem(dest, bps) * bw, bw), bw)]
 
     def b_copy(dest, src):
         return pltpu.make_async_remote_copy(
-            src_ref=b_src(dest), dst_ref=blocks.at[src],
+            src_ref=b_src(dest, zr, tok - zr), dst_ref=blocks.at[src, pl.ds(zr, tok - zr)],
             send_sem=b_send.at[dest], recv_sem=b_recv.at[src],
             device_id=(dest, t), device_id_type=MESH,
         )
+
+    def q_copy(dest, src):
+        row = pl.multiple_of(t * share, 16)
+        return pltpu.make_async_remote_copy(
+            src_ref=b_src(dest, row, share), dst_ref=blocks.at[src, pl.ds(row, share)],
+            send_sem=q_send.at[dest], recv_sem=q_recv.at[src],
+            device_id=(dest, t), device_id_type=MESH,
+        )
+
+    def own_block():
+        return pltpu.make_async_copy(b_src(s, zr, tok - zr), blocks.at[s, pl.ds(zr, tok - zr)], b_recv.at[s])
+
+    def own_quarter():
+        row = pl.multiple_of(t * share, 16)
+        return pltpu.make_async_copy(b_src(s, row, share), blocks.at[s, pl.ds(row, share)], q_recv.at[s])
+
+    def y_copy(way, hop, k, dest):
+        rows = pl.ds(pl.multiple_of(k * share, 16), share)
+        return pltpu.make_async_remote_copy(
+            src_ref=blocks.at[:, rows], dst_ref=blocks.at[:, rows],
+            send_sem=y_send.at[way, hop], recv_sem=y_recv.at[way, hop],
+            device_id=(s, dest), device_id_type=MESH,
+        )
+
+    def y_step(hop):
+        for way in range(2):
+            k = t - hop if way == 0 else t + hop
+            here = k >= 0 if way == 0 else k < tensors
+            onward = up_ok if way == 0 else dn_ok
+            dest = t + 1 if way == 0 else t - 1
+
+            @pl.when(jnp.logical_and(hop > 0, here))
+            def _():
+                y_copy(way, hop, k, t).wait_recv()
+
+            @pl.when(jnp.logical_and(here, onward))
+            def _():
+                y_copy(way, hop + 1, k, dest).start()
 
     def own_copy(k):
         rows = pl.ds(pl.multiple_of(s * cap, cap), cap)
@@ -296,6 +338,7 @@
             return c
 
         lax.fori_loop(1, tensors, send_t, 0)
+        y_step(tensors - 2)
 
         def take_t(r, c):
             t_copy(t, lax.rem(t + r, tensors)).wait_recv()
@@ -397,6 +440,16 @@
         def _():
             arrive(hop)
 
+        @pl.when(hop == tensors - 1)
+        def _():
+            own_quarter().start()
+
+            def send(r, c):
+                q_copy(lax.rem(s + r, sections), s).start()
+                return c
+
+            lax.fori_loop(1, sections, send, 0)
+
         def inner(way, c):
             k = jnp.where(way == 0, t - hop, t + hop)
             fine = jnp.logical_and(jnp.logical_and(k >= 0, k < tensors), jnp.logical_or(hop > 0, way == 0))
@@ -413,8 +466,24 @@
         @pl.when(hop == tensors - 1)
         def _():
             hidden_step()
-            pltpu.make_async_copy(b_src(s), blocks.at[s], b_recv.at[s]).start()
+            own_block().start()
             lax.fori_loop(1, sections - spare, send_block, 0)
+            own_quarter().wait()
+
+            def take(r, c):
+                q_copy(s, lax.rem(s + r, sections)).wait_recv()
+                return c
+
+            lax.fori_loop(1, sections, take, 0)
+            y_step(0)
+
+        @pl.when(hop == tensors)
+        def _():
+            def onward(h, c):
+                y_step(h)
+                return c
+
+            lax.fori_loop(1, tensors - 2, onward, 0)
 
         def inner_m(way, c):
             k = jnp.where(way == 0, t - (hop - 1), t + (hop - 1))
@@ -433,12 +502,14 @@
     score_step()
     settle()
 
-    pltpu.make_async_copy(b_src(s), blocks.at[s], b_recv.at[s]).wait()
+    own_block().wait()
+    y_step(tensors - 1)
 
     def finish(r, c):
         other = lax.rem(s + r, sections)
         b_copy(s, other).wait_recv()
         b_copy(other, s).wait_send()
+        q_copy(other, s).wait_send()
 
         def sent(k, c):
             m_copy(k, other, s).wait_send()
@@ -449,6 +520,14 @@
     lax.fori_loop(1, sections, finish, 0)
 
     def drain(hop, c):
+        @pl.when(jnp.logical_and(t - hop >= 0, up_ok))
+        def _():
+            y_copy(0, hop + 1, t - hop, t + 1).wait_send()
+
+        @pl.when(jnp.logical_and(t + hop < tensors, dn_ok))
+        def _():
+            y_copy(1, hop + 1, t + hop, t - 1).wait_send()
+
         for cc in range(chunks):
             @pl.when(jnp.logical_and(t - hop >= 0, up_ok))
             def _():
@@ -534,6 +613,10 @@
             pltpu.SemaphoreType.DMA((sections,)),
             pltpu.SemaphoreType.DMA((sections,)),
             pltpu.SemaphoreType.DMA((sections,)),
+            pltpu.SemaphoreType.DMA((sections,)),
+            pltpu.SemaphoreType.DMA((sections,)),
+            pltpu.SemaphoreType.DMA((2, tensors + 1)),
+            pltpu.SemaphoreType.DMA((2, tensors + 1)),
         ],
         compiler_params=pltpu.CompilerParams(
             collective_id=0, has_side_effects=True, vmem_limit_bytes=67043328

time: 368 us -> 347 us (0.943)
  Pallas kernels: 337 us -> 314 us
    pallas_call x1, Pallas kernels: 337 us -> 314 us  [body(): pl.pallas_call(functools.partial(exchange, sections, tensors, cap), out_s...]
where the time goes in v3:
time: 347 us; the launch traced here: 344 us
  Pallas kernels  314 us (90%)
  matrix products  15.5 us (4%)
  other arithmetic  8.38 us (2%)
    pallas_call x1, Pallas kernels, body(): pl.pallas_call(functools.partial(exchange, sections, tensors, cap), out_s...  314 us
    dot_general x1, matrix products, body(): lax.dot_general(left, right, (((0,), (0,)), ((), ())), preferred_element_...  15.5 us

profile of v3, /device:TPU:0, one launch (start us, length us, event | category | flops | bytes accessed | tf_op | source)
XLA Modules:
  0.0 343.5 jit_solution(17911863991996064563)
XLA Ops:
  0.6 0.7 select_reduce_fusion
  1.4 0.1 fusion.6
  1.5 0.6 convert_element_type.43
  2.1 1.0 convert_reduce_fusion
  3.1 0.7 multiply_add_fusion
  3.8 1.3 dynamic_slice.8
  5.0 1.4 fusion.4.dispatch
  6.4 313.7 %shard_map.112 = (f32[8,8,128]{2,1,0:T(8,128)}, f32[8,8,512]{2,1,0:T(8,128)}, bf16[8,512,1024]{2,1,0:T(8,128)(2,1)}, bf16[8,512,1024]{2,1,0:T(8,128)(2,1)}) custom-call(bf16[512,2048]{1,0:T(8,128)(2,1)} %states.1, bf16[1024,512]{1,0:T(8,128)(2,1)} %fusion.4.dispatch, f32[4,1,2048]{2,1,0:T(1,128)} %bitcast.22, f32[4,1,2048]{2,1,0:T(1,128)} %bitcast.21, ...), custom_call_target="tpu_custom_call" | custom-call | tf_op jit(solution)/shard_map/pallas_call | solution.py:571
  320.1 1.4 slice_bitcast_fusion
  321.5 1.5 slice_reduce_fusion
  325.7 1.3 fusion.7
  327.0 1.0 multiply_subtract_fusion
  328.0 15.5 %fusion.3 = f32[1024,1024]{1,0:T(8,128)} fusion(bf16[8,512,1024]{2,1,0:T(8,128)(2,1)} %get-tuple-element.10, f32[8,512]{1,0:T(8,128)S(1)} %bitcast.25, bf16[8,512,1024]{2,1,0:T(8,128)(2,1)} %get-tuple-element.9, f32[1024]{0:T(1024)} %dynamic_slice.8), kind=kOutput, calls=%fused_computation.5 | convolution fusion | flops 8615100416 | bytes 20992000 | tf_op jit(solution)/shard_map/dot_general | solution.py:644
  (2 shorter events, 0.0 us)
